TPU v7x, 32 devices: a whole 2x2x4 slice. The times are simulated.
32 devices in a mesh: blk: 8 (over z, y), exp: 4 (over x, core).
Axes of the slice: x: 2, y: 2, z: 4, core: 2. Of those that a mesh axis runs over, the one named last changes fastest.
Arguments:
- grad_block: bfloat16 [128, 256, 2048], P('exp', 'blk'), may hold values from -6 to 6
- momentum: float32 [128, 256, 2048], P('exp', 'blk'), may hold values from -6 to 6
- model_root: bfloat16 [2048, 2048], P('blk'), may hold values from -0.125 to 0.125
- expert_root: bfloat16 [128, 128], replicated, may hold values from -0.5 to 0.5
Outputs:
- momentum_new: float32 [128, 256, 2048], P('exp', 'blk')
All inputs are finite; a program needn't handle non-finite values.
Results may differ from a plain program's by a relative error of at most 0.0031.
Values may be sent and summed in bfloat16 or wider, within the bound.
A program may use at most 128 MiB of HBM per device.

v0:
```python
import jax
import jax.numpy as jnp
from jax import lax
from jax.sharding import PartitionSpec as P


def per_device(grad_block, momentum, model_root, expert_root):
    local_experts, local_hidden, width = grad_block.shape
    flat_rows = grad_block.reshape(local_experts * local_hidden, width)
    sub_rows = model_root.shape[0] // lax.axis_size("exp")
    sliver = lax.dynamic_slice_in_dim(model_root, lax.axis_index("exp") * sub_rows, sub_rows, 0)
    whole_root = lax.all_gather(sliver, ("blk", "exp"), axis=0, tiled=True)
    products = lax.dot_general(
        flat_rows, whole_root, (((1,), (1,)), ((), ())), preferred_element_type=jnp.float32
    )
    model_mode = products.astype(jnp.bfloat16).reshape(local_experts, local_hidden, width)
    swapped = lax.all_to_all(model_mode, "exp", split_axis=2, concat_axis=0, tiled=True)
    all_experts, items, columns = swapped.shape
    blended = jnp.dot(
        expert_root,
        swapped.reshape(all_experts, items * columns),
        preferred_element_type=jnp.float32,
    )
    blended = blended.astype(jnp.bfloat16).reshape(all_experts, items, columns)
    restored = lax.all_to_all(blended, "exp", split_axis=0, concat_axis=2, tiled=True)
    return 0.9 * momentum + restored.astype(jnp.float32)


def solution(mesh):
    placed = (P("exp", "blk", None), P("exp", "blk", None), P("blk", None), P())
    return jax.shard_map(
        per_device, mesh=mesh, in_specs=placed, out_specs=P("exp", "blk", None), check_vma=False
    )
```

profile of v0, /device:TPU:0, one launch (start us, length us, event | category | flops | bytes accessed | tf_op | source)
XLA Modules:
  0.0 324.6 jit_solution(5379010461249229389)
XLA Ops:
  6.5 0.0 copy-start
  6.5 0.0 all-gather.2.cloned.1.call-start
  6.5 1.2 copy-done
  7.8 0.7 constant_dynamic-slice_fusion
  8.5 0.0 all-gather.2.cloned.1.call-update
  8.5 81.5 %all-gather.2.cloned.1.call-done = bf16[2048,2048]{1,0:T(8,128)(2,1)} async-done(((bf16[64,2048]{1,0:T(8,128)(2,1)}), bf16[2048,2048]{1,0:T(8,128)(2,1)}) %all-gather.2.cloned.1.call-update) | async-done | bytes 8388624 | tf_op jit(solution)/shard_map/all_gather | solution.py:12
  90.0 13.9 %convolution_convert_fusion.1 = bf16[2048,1024]{0,1:T(8,128)(2,1)} fusion(bf16[2048,2048]{1,0:T(8,128)(2,1)} %all-gather.2.cloned.1.call-done, bf16[1024,2048]{1,0:T(8,128)(2,1)} %bitcast.33), kind=kOutput, calls=%fused_computation.3 | convolution fusion | flops 8592031744 | bytes 16777216 | tf_op jit(solution)/shard_map/dot_general | solution.py:13
  103.8 23.0 %copy.10 = bf16[32,32,2048]{1,0,2:T(8,128)(2,1)} copy(bf16[32,32,2048]{2,1,0:T(8,128)(2,1)} %bitcast.32) | data formatting | bytes 8388608 | tf_op jit(solution)/shard_map/reshape | solution.py:16
  126.9 19.2 %reshape.23 = bf16[4,2,262144]{2,1,0:T(2,128)(2,1)} reshape(bf16[2048,32,32]{2,1,0:T(8,128)(2,1)} %bitcast.24) | data formatting | bytes 8388608
  146.1 53.8 %all_to_all.24 = bf16[4,2,262144]{2,1,0:T(2,128)(2,1)} all-to-all(bf16[4,2,262144]{2,1,0:T(2,128)(2,1)} %reshape.23), channel_id=1, replica_groups=mesh['blk'=8,'exp'=4] {'exp'}, dimensions={0} | all-to-all | bytes 8388608 | tf_op jit(solution)/shard_map/all_to_all | solution.py:17
  199.9 12.0 %reshape.24 = bf16[2048,32,32]{2,1,0:T(8,128)(2,1)} reshape(bf16[4,2,262144]{2,1,0:T(2,128)(2,1)} %all_to_all.24) | data formatting | bytes 8388608
  211.9 18.8 %copy.15 = bf16[32,32,4,512]{3,2,1,0:T(4,128)(2,1)} copy(bf16[32,32,4,512]{1,0,3,2:T(8,128)(2,1)} %bitcast.25) | data formatting | bytes 8388608 | tf_op jit(solution)/shard_map/all_to_all | solution.py:17
  230.7 3.2 copy.12
  233.9 0.0 copy-start.2
  233.9 2.9 copy.17
  236.8 0.0 copy-done.2
  236.8 3.3 %convolution_convert_fusion = bf16[16384,128]{1,0:T(8,128)(2,1)} fusion(bf16[128,16384]{1,0:T(8,128)(2,1)S(1)} %bitcast.27, bf16[128,128]{1,0:T(8,128)(2,1)S(1)} %copy-done.2), kind=kOutput, calls=%fused_computation | convolution fusion | flops 538968064 | bytes 8421376 | tf_op jit(solution)/shard_map/dot_general | solution.py:19
  240.2 8.0 %copy.13 = bf16[128,32,512]{2,1,0:T(8,128)(2,1)} copy(bf16[128,32,512]{0,2,1:T(8,128)(2,1)} %bitcast.28) | data formatting | bytes 8388608 | tf_op jit(solution)/shard_map/reshape | solution.py:24
  248.1 51.9 %all_to_all.25 = bf16[128,32,512]{2,1,0:T(8,128)(2,1)S(1)} all-to-all(bf16[128,32,512]{2,1,0:T(8,128)(2,1)} %copy.13), channel_id=1, replica_groups=mesh['blk'=8,'exp'=4] {'exp'}, dimensions={0} | all-to-all | bytes 8388608 | tf_op jit(solution)/shard_map/all_to_all | solution.py:25
  300.0 1.2 convert_bitcast_fusion
  301.3 4.4 %copy.16 = f32[4,32,4,8,512]{4,3,0,2,1:T(8,128)} copy(f32[4,32,4,8,512]{4,3,2,1,0:T(8,128)S(1)} %convert_bitcast_fusion) | data formatting | bytes 16777216 | tf_op jit(solution)/shard_map/convert_element_type | solution.py:26
  305.7 0.0 copy-start.1
  305.7 12.1 %multiply_add_fusion = f32[32,32,2048]{2,1,0:T(8,128)} fusion(f32[32,32,2048]{2,1,0:T(8,128)} %bitcast.26, f32[32,32,2048]{2,1,0:T(8,128)} %param.5), kind=kLoop, calls=%fused_computation.2 | loop fusion | flops 4194304 | bytes 25165824 | tf_op jit(solution)/shard_map/add | solution.py:26
  317.8 0.0 copy-done.1
Async XLA Ops:
  6.5 1.2 copy-start
  6.5 83.5 %all-gather.2.cloned.1.call-start = ((), (), s32[]{:S(2)}) async-start(), calls=%async_computation.2 | async-start | bytes 8650752 | tf_op jit(solution)/shard_map/all_gather | solution.py:12
  233.9 2.9 copy-start.2
  305.7 12.1 %copy-start.1 = (bf16[256,2048]{1,0:T(8,128)(2,1)S(1)}, bf16[256,2048]{1,0:T(8,128)(2,1)}, u32[]{:S(2)}) copy-start(bf16[256,2048]{1,0:T(8,128)(2,1)} %param.6) | copy-start | bytes 3145732
Sparse Core Ops, SparseCore 0:
  10.2 79.7 all-gather.1
where the time goes:
time: 326 us; the launch traced here: 325 us
  blocking collectives  106 us (33%)
  local copies, waits for them, and re-layouts  93.5 us (29%)
  waiting for transfers between devices  81.5 us (25%)
  matrix products  17.2 us (5%)
  between operations  13.4 us (4%)
  other arithmetic  13.3 us (4%)
    all_gather x1, waiting for transfers between devices, per_device(): whole_root = lax.all_gather(sliver, ('blk', 'exp'), axis=0, tiled=True)  81.5 us
    all_to_all x1, blocking collectives, per_device(): lax.all_to_all(model_mode, 'exp', split_axis=2, concat_axis=0, tiled=True)  53.8 us
    all_to_all x1, blocking collectives, per_device(): lax.all_to_all(blended, 'exp', split_axis=0, concat_axis=2, tiled=True)  51.9 us
    unnamed x9, local copies, waits for them, and re-layouts  35.3 us
    reshape x1, local copies, waits for them, and re-layouts, per_device(): products.astype(jnp.bfloat16).reshape(local_experts, local_hidden, width)  23 us
    all_to_all x2, local copies, waits for them, and re-layouts, per_device(): lax.all_to_all(model_mode, 'exp', split_axis=2, concat_axis=0, tiled=True)  22 us
    dot_general x1, matrix products, per_device(): lax.dot_general(flat_rows, whole_root, (((1,), (1,)), ((), ())), preferre...  13.9 us
    add x1, other arithmetic, per_device(): return 0.9 * momentum + restored.astype(jnp.float32)  12.1 us
  transfers between devices with their start and end apart: 1, of which 1 were waited for; matrix products, arithmetic and copies ran while one was open for 0% of the time, Pallas kernels for 0%

commit v1 on v0

v1 whole, which is shorter than its diff:
```python
import functools

import jax
import jax.numpy as jnp
from jax import lax
from jax.experimental import pallas as pl
from jax.experimental.pallas import tpu as pltpu
from jax.sharding import PartitionSpec as P

MESH = pl.DeviceIdType.MESH
SUB = 16
TILE = 256


def kernel(
    n_blk, n_exp, n_chunks,
    grad, momentum, root_rows, expert_root, out,
    gathered, root, mix, blended, total,
    x_send, x_recv, p_send, p_recv, f_send, f_recv, own_sem,
    z_send, z_recv, y_send, y_recv, c_send, c_recv, root_sem, mom_sem, out_sem,
):
    local_experts, local_hidden, width = grad.shape
    groups = local_hidden // SUB
    chunk = width // n_chunks
    chips = n_exp // 2
    n_z = n_blk // 2
    rows = local_experts * SUB
    half = root.shape[2]
    slice_rows = 2 * half

    me = lax.axis_index("exp")
    chip, core = me // 2, me % 2
    blk = lax.axis_index("blk")
    zi, yi = blk // 2, blk % 2
    mate = {"exp": chip * 2 + 1 - core}
    y_peer = {"blk": zi * 2 + 1 - yi}

    def chip_at(offset):
        return lax.rem(chip + offset + chips, chips)

    def z_at(offset):
        return lax.rem(zi + offset + n_z, n_z)

    def remote(src, dst, send, recv, device):
        return pltpu.make_async_remote_copy(
            src_ref=src, dst_ref=dst, send_sem=send, recv_sem=recv, device_id=device, device_id_type=MESH
        )

    barrier = pltpu.get_barrier_semaphore()
    peers = [mate, y_peer]
    peers += [{"exp": chip_at(c) * 2 + core} for c in range(1, chips)]
    peers += [{"blk": z_at(d) * 2 + yi} for d in range(1, n_z)]
    for peer in peers:
        pl.semaphore_signal(barrier, inc=1, device_id=peer, device_id_type=MESH)
    pl.semaphore_wait(barrier, len(peers))

    pieces = [(g, c) for g in range(groups) for c in range(n_chunks)]
    grad_at = [grad.at[:, pl.ds(g * SUB, SUB), pl.ds(c * chunk, chunk)] for g, c in pieces]

    def x_copy(p, off):
        slot = gathered.at[p, me]
        return remote(grad_at[p], slot, x_send.at[p, off - 1], x_recv.at[p, off - 1], {"exp": chip_at(off) * 2 + core})

    def p_copy(p):
        return remote(grad_at[p], gathered.at[p, me], p_send.at[p], p_recv.at[p], mate)

    def f_copy(p, off):
        slot = gathered.at[p, chip_at(-off) * 2 + core]
        return remote(slot, slot, f_send.at[p, off - 1], f_recv.at[p, off - 1], mate)

    def own_copy(p):
        return pltpu.make_async_copy(grad_at[p], gathered.at[p, me], own_sem.at[p])

    own_half = root_rows.at[core]

    def z_copy(d):
        return remote(own_half, root.at[blk, core], z_send.at[d - 1], z_recv.at[d - 1], {"blk": z_at(d) * 2 + yi})

    def y_copy(d):
        slot = root.at[z_at(-d) * 2 + yi, core]
        return remote(own_half if d == 0 else slot, slot, y_send.at[d], y_recv.at[d], y_peer)

    def c_copy(side, d):
        slot = root.at[z_at(-d) * 2 + (yi if side == 0 else 1 - yi), core]
        return remote(slot, slot, c_send.at[side, d], c_recv.at[side, d], mate)

    root_own = pltpu.make_async_copy(root_rows, root.at[blk], root_sem)

    def mom_copy(g):
        return pltpu.make_async_copy(momentum.at[:, pl.ds(g * SUB, SUB), :], total.at[g], mom_sem.at[g])

    def out_copy(g, b):
        cols = pl.ds(pl.multiple_of(b * slice_rows, slice_rows), slice_rows)
        return pltpu.make_async_copy(
            total.at[g, :, :, cols], out.at[:, pl.ds(g * SUB, SUB), cols], out_sem.at[g, b]
        )

    for off in range(1, chips):
        x_copy(0, off).start()
    y_copy(0).start()
    for d in range(1, n_z):
        z_copy(d).start()
    for p in range(1, len(pieces)):
        for off in range(1, chips):
            x_copy(p, off).start()
    for p in range(len(pieces)):
        own_copy(p).start()
        p_copy(p).start()
    root_own.start()
    for g in range(groups):
        mom_copy(g).start()

    experts = expert_root.shape[1]
    spread = lax.broadcasted_iota(jnp.int32, (rows, local_experts), 0) // SUB
    spread = spread == lax.broadcasted_iota(jnp.int32, (rows, local_experts), 1)
    mine = expert_root[pl.ds(pl.multiple_of(me * local_experts, local_experts), local_experts), :]
    tall = jnp.dot(jnp.where(spread, 1.0, 0.0).astype(jnp.bfloat16), mine, preferred_element_type=jnp.float32)
    tall = tall.astype(jnp.bfloat16)

    @pl.loop(0, experts * SUB // TILE)
    def _(t):
        col = t * TILE + lax.broadcasted_iota(jnp.int32, (experts, TILE), 1)
        pick = col // SUB == lax.broadcasted_iota(jnp.int32, (experts, TILE), 0)
        wide = jnp.dot(tall, jnp.where(pick, 1.0, 0.0).astype(jnp.bfloat16), preferred_element_type=jnp.float32)
        same = lax.broadcasted_iota(jnp.int32, (rows, TILE), 0) % SUB == lax.broadcasted_iota(
            jnp.int32, (rows, TILE), 1) % SUB
        mix[:, pl.ds(pl.multiple_of(t * TILE, TILE), TILE)] = jnp.where(same, wide, 0.0).astype(jnp.bfloat16)

    for g in range(groups):
        mom_copy(g).wait()

        @pl.loop(0, local_experts)
        def _(e):
            total[g, e] = 0.9 * total[g, e]

    def blend(p):
        g, c = pieces[p]

        @pl.loop(0, chunk // TILE)
        def _(t):
            block = gathered[p, :, :, :, pl.ds(pl.multiple_of(t * TILE, TILE), TILE)]
            block = block.reshape(experts * SUB, TILE)
            cols = pl.ds(pl.multiple_of(c * chunk + t * TILE, TILE), TILE)
            blended[g, :, cols] = jnp.dot(
                mix[...], block, preferred_element_type=jnp.float32
            ).astype(jnp.bfloat16)

    def apply_root(g, first, last):
        cols = pl.ds(first * chunk, (last - first) * chunk)

        @pl.loop(0, n_blk)
        def _(b):
            taps = root[b, :, :, cols].reshape(slice_rows, (last - first) * chunk)
            part = lax.dot_general(
                blended[g, :, cols], taps, (((1,), (1,)), ((), ())), preferred_element_type=jnp.float32
            )
            dst = pl.ds(pl.multiple_of(b * slice_rows, slice_rows), slice_rows)
            total[g, :, :, dst] += part.reshape(local_experts, SUB, slice_rows)
            if last == n_chunks:
                out_copy(g, b).start()

    def take_z(d):
        z_copy(d).wait_recv()
        y_copy(d).start()
        c_copy(0, d).start()

    def take_y(d):
        y_copy(d).wait_recv()
        c_copy(1, d).start()

    events = [functools.partial(take_z, d) for d in range(1, n_z)]
    events += [functools.partial(take_y, d) for d in range(n_z)]
    ready = len(pieces) * 5 // 8
    done = 0
    pending = 0
    for p, (g, c) in enumerate(pieces):
        for off in range(1, chips):
            x_copy(p, off).wait_recv()
            f_copy(p, off).start()
        goal = len(events) if p >= ready else len(events) * (p + 1) // (ready + 1)
        for event in events[done:goal]:
            event()
        done = goal
        own_copy(p).wait()
        p_copy(p).wait_recv()
        for off in range(1, chips):
            f_copy(p, off).wait_recv()
        blend(p)
        if p == ready:
            root_own.wait()
            for d in range(n_z):
                if d:
                    c_copy(0, d).wait_recv()
                c_copy(1, d).wait_recv()
        if p >= ready:
            while pending <= p:
                gg, first = pieces[pending]
                last = c + 1 if gg == g else n_chunks
                apply_root(gg, first, last)
                pending += last - first

    for p in range(len(pieces)):
        p_copy(p).wait_send()
        for off in range(1, chips):
            x_copy(p, off).wait_send()
            f_copy(p, off).wait_send()
    for d in range(n_z):
        y_copy(d).wait_send()
        c_copy(1, d).wait_send()
        if d:
            z_copy(d).wait_send()
            c_copy(0, d).wait_send()
    for g in range(groups):

        @pl.loop(0, n_blk)
        def _(b):
            out_copy(g, b).wait()


def solution(mesh):
    n_blk, n_exp = mesh.shape["blk"], mesh.shape["exp"]

    def per_device(grad_block, momentum, model_root, expert_root):
        local_experts, local_hidden, width = grad_block.shape
        experts = expert_root.shape[0]
        groups, n_chunks = local_hidden // SUB, 4
        pieces, rows = groups * n_chunks, local_experts * SUB
        half = model_root.shape[0] // 2
        chips, n_z = n_exp // 2, n_blk // 2
        dma = pltpu.SemaphoreType.DMA
        hbm = pl.BlockSpec(memory_space=pl.ANY)
        return pl.pallas_call(
            functools.partial(kernel, n_blk, n_exp, n_chunks),
            out_shape=jax.ShapeDtypeStruct(momentum.shape, jnp.float32),
            in_specs=[hbm, hbm, hbm, pl.BlockSpec(memory_space=pltpu.VMEM)],
            out_specs=hbm,
            scratch_shapes=[
                pltpu.VMEM((pieces, n_exp, local_experts, SUB, width // n_chunks), jnp.bfloat16),
                pltpu.VMEM((n_blk, 2, half, width), jnp.bfloat16),
                pltpu.VMEM((rows, experts * SUB), jnp.bfloat16),
                pltpu.VMEM((groups, rows, width), jnp.bfloat16),
                pltpu.VMEM((groups, local_experts, SUB, width), jnp.float32),
                dma((pieces, chips - 1)), dma((pieces, chips - 1)),
                dma((pieces,)), dma((pieces,)),
                dma((pieces, chips - 1)), dma((pieces, chips - 1)),
                dma((pieces,)),
                dma((n_z - 1,)), dma((n_z - 1,)),
                dma((n_z,)), dma((n_z,)),
                dma((2, n_z)), dma((2, n_z)),
                dma, dma((groups,)), dma((groups, n_blk)),
            ],
            compiler_params=pltpu.CompilerParams(
                collective_id=0, has_side_effects=True, vmem_limit_bytes=67_043_328
            ),
        )(grad_block, momentum, model_root.reshape(2, half, width), expert_root)

    placed = (P("exp", "blk", None), P("exp", "blk", None), P("blk", None), P())
    return jax.shard_map(
        per_device, mesh=mesh, in_specs=placed, out_specs=P("exp", "blk", None), check_vma=False
    )
```

time: 326 us -> 113 us (0.35)
  blocking collectives: 106 us -> 0 us
  Pallas kernels: 0 us -> 104 us
  local copies, waits for them, and re-layouts: 93.5 us -> 7.89 us
  waiting for transfers between devices: 81.5 us -> 0 us
  matrix products: 17.2 us -> 0 us
  between operations: 13.4 us -> 0.01 us
  other arithmetic: 13.3 us -> 0 us
    all_to_all x2 -> x0, blocking collectives: 106 us -> none  [the longest x1 53.8 us: per_device(): lax.all_to_all(model_mode, 'exp', split_axis=2, concat_axis=0, tiled=True)]
    pallas_call x0 -> x1, Pallas kernels: none -> 104 us  [per_device(): pl.pallas_call(functools.partial(kernel, n_blk, n_exp, n_chunks), out_sha...]
    all_gather x1 -> x0, waiting for transfers between devices: 81.5 us -> none  [per_device(): whole_root = lax.all_gather(sliver, ('blk', 'exp'), axis=0, tiled=True)]
    reshape x2 -> x0, local copies, waits for them, and re-layouts: 31 us -> none  [the longest x1 23 us: per_device(): products.astype(jnp.bfloat16).reshape(local_experts, local_hidden, width)]
    unnamed x9 -> x1, local copies, waits for them, and re-layouts: 35.3 us -> 7.89 us
    all_to_all x2 -> x0, local copies, waits for them, and re-layouts: 22 us -> none  [per_device(): lax.all_to_all(model_mode, 'exp', split_axis=2, concat_axis=0, tiled=True)]
    dot_general x2 -> x0, matrix products: 17.2 us -> none  [the longest x1 13.9 us: per_device(): lax.dot_general(flat_rows, whole_root, (((1,), (1,)), ((), ())), preferre...]
    add x1 -> x0, other arithmetic: 12.1 us -> none  [per_device(): return 0.9 * momentum + restored.astype(jnp.float32)]
  transfers between devices with their start and end apart: 1 -> 0, of which waited for: 1 -> 0; matrix products, arithmetic and copies ran while one was open for 0% -> 0% of each run, Pallas kernels for 0% -> 0%
where the time goes in v1:
time: 113 us; the launch traced here: 112 us
  Pallas kernels  104 us (92%)
  local copies, waits for them, and re-layouts  7.89 us (7%)
    pallas_call x1, Pallas kernels, per_device(): pl.pallas_call(functools.partial(kernel, n_blk, n_exp, n_chunks), out_sha...  104 us
    unnamed x1, local copies, waits for them, and re-layouts  7.89 us

profile of v1, /device:TPU:0, one launch (start us, length us, event | category | flops | bytes accessed | tf_op | source)
XLA Modules:
  0.0 112.0 jit_solution(1656953542410812911)
XLA Ops:
  0.0 104.1 %shard_map.46 = f32[32,32,2048]{2,1,0:T(8,128)} custom-call(bf16[32,32,2048]{2,1,0:T(8,128)(2,1)} %grad.1, f32[32,32,2048]{2,1,0:T(8,128)} %momentum.1, bf16[2,128,2048]{2,1,0:T(8,128)(2,1)} %bitcast.1, bf16[128,128]{1,0:T(8,128)(2,1)} %expert_root.1), custom_call_target="tpu_custom_call" | custom-call | tf_op jit(solution)/shard_map/pallas_call | solution.py:232
  104.1 7.9 %copy.6 = f32[32,32,2048]{2,1,0:T(8,128)} copy(f32[32,32,2048]{2,1,0:T(8,128)} %shard_map.46) | data formatting | bytes 16777216

commit v2 on v1

--- a/solution.py
+++ b/solution.py
@@ -15,9 +15,9 @@
 def kernel(
     n_blk, n_exp, n_chunks,
     grad, momentum, root_rows, expert_root, out,
-    gathered, root, mix, blended, total,
+    gathered, root, mix, blended,
     x_send, x_recv, p_send, p_recv, f_send, f_recv, own_sem,
-    z_send, z_recv, y_send, y_recv, c_send, c_recv, root_sem, mom_sem, out_sem,
+    z_send, z_recv, y_send, y_recv, c_send, c_recv, root_sem, mom_sem,
 ):
     local_experts, local_hidden, width = grad.shape
     groups = local_hidden // SUB
@@ -26,6 +26,8 @@
     n_z = n_blk // 2
     rows = local_experts * SUB
     half = root.shape[2]
+    batch = 4 if n_exp % 4 == 0 else 2
+    depth = batch * rows
     slice_rows = 2 * half
 
     me = lax.axis_index("exp")
@@ -87,13 +89,8 @@
     root_own = pltpu.make_async_copy(root_rows, root.at[blk], root_sem)
 
     def mom_copy(g):
-        return pltpu.make_async_copy(momentum.at[:, pl.ds(g * SUB, SUB), :], total.at[g], mom_sem.at[g])
-
-    def out_copy(g, b):
-        cols = pl.ds(pl.multiple_of(b * slice_rows, slice_rows), slice_rows)
-        return pltpu.make_async_copy(
-            total.at[g, :, :, cols], out.at[:, pl.ds(g * SUB, SUB), cols], out_sem.at[g, b]
-        )
+        cols = pl.ds(g * SUB, SUB)
+        return pltpu.make_async_copy(momentum.at[:, cols, :], out.at[:, cols, :], mom_sem.at[g])
 
     for off in range(1, chips):
         x_copy(0, off).start()
@@ -131,19 +128,25 @@
 
         @pl.loop(0, local_experts)
         def _(e):
-            total[g, e] = 0.9 * total[g, e]
+            out[e, pl.ds(g * SUB, SUB)] = 0.9 * out[e, pl.ds(g * SUB, SUB)]
 
     def blend(p):
         g, c = pieces[p]
 
         @pl.loop(0, chunk // TILE)
         def _(t):
-            block = gathered[p, :, :, :, pl.ds(pl.multiple_of(t * TILE, TILE), TILE)]
-            block = block.reshape(experts * SUB, TILE)
+            lanes = pl.ds(pl.multiple_of(t * TILE, TILE), TILE)
             cols = pl.ds(pl.multiple_of(c * chunk + t * TILE, TILE), TILE)
-            blended[g, :, cols] = jnp.dot(
-                mix[...], block, preferred_element_type=jnp.float32
-            ).astype(jnp.bfloat16)
+
+            def term(k):
+                block = gathered[p, pl.ds(k * batch, batch), :, :, lanes].reshape(depth, TILE)
+                taps = mix[:, pl.ds(pl.multiple_of(k * depth, depth), depth)]
+                return jnp.dot(taps, block, preferred_element_type=jnp.float32)
+
+            acc = term(0)
+            if n_exp > batch:
+                acc = lax.fori_loop(1, n_exp // batch, lambda k, a: a + term(k), acc)
+            blended[g, :, cols] = acc.astype(jnp.bfloat16)
 
     def apply_root(g, first, last):
         cols = pl.ds(first * chunk, (last - first) * chunk)
@@ -155,9 +158,7 @@
                 blended[g, :, cols], taps, (((1,), (1,)), ((), ())), preferred_element_type=jnp.float32
             )
             dst = pl.ds(pl.multiple_of(b * slice_rows, slice_rows), slice_rows)
-            total[g, :, :, dst] += part.reshape(local_experts, SUB, slice_rows)
-            if last == n_chunks:
-                out_copy(g, b).start()
+            out[:, pl.ds(g * SUB, SUB), dst] += part.reshape(local_experts, SUB, slice_rows)
 
     def take_z(d):
         z_copy(d).wait_recv()
@@ -210,11 +211,6 @@
         if d:
             z_copy(d).wait_send()
             c_copy(0, d).wait_send()
-    for g in range(groups):
-
-        @pl.loop(0, n_blk)
-        def _(b):
-            out_copy(g, b).wait()
 
 
 def solution(mesh):
@@ -223,7 +219,7 @@
     def per_device(grad_block, momentum, model_root, expert_root):
         local_experts, local_hidden, width = grad_block.shape
         experts = expert_root.shape[0]
-        groups, n_chunks = local_hidden // SUB, 4
+        groups, n_chunks = local_hidden // SUB, 8
         pieces, rows = groups * n_chunks, local_experts * SUB
         half = model_root.shape[0] // 2
         chips, n_z = n_exp // 2, n_blk // 2
@@ -231,15 +227,14 @@
         hbm = pl.BlockSpec(memory_space=pl.ANY)
         return pl.pallas_call(
             functools.partial(kernel, n_blk, n_exp, n_chunks),
-            out_shape=jax.ShapeDtypeStruct(momentum.shape, jnp.float32),
+            out_shape=pltpu.VMEM(momentum.shape, jnp.float32),
             in_specs=[hbm, hbm, hbm, pl.BlockSpec(memory_space=pltpu.VMEM)],
-            out_specs=hbm,
+            out_specs=pl.BlockSpec(memory_space=pltpu.VMEM),
             scratch_shapes=[
                 pltpu.VMEM((pieces, n_exp, local_experts, SUB, width // n_chunks), jnp.bfloat16),
                 pltpu.VMEM((n_blk, 2, half, width), jnp.bfloat16),
                 pltpu.VMEM((rows, experts * SUB), jnp.bfloat16),
                 pltpu.VMEM((groups, rows, width), jnp.bfloat16),
-                pltpu.VMEM((groups, local_experts, SUB, width), jnp.float32),
                 dma((pieces, chips - 1)), dma((pieces, chips - 1)),
                 dma((pieces,)), dma((pieces,)),
                 dma((pieces, chips - 1)), dma((pieces, chips - 1)),
@@ -247,10 +242,10 @@
                 dma((n_z - 1,)), dma((n_z - 1,)),
                 dma((n_z,)), dma((n_z,)),
                 dma((2, n_z)), dma((2, n_z)),
-                dma, dma((groups,)), dma((groups, n_blk)),
+                dma, dma((groups,)),
             ],
             compiler_params=pltpu.CompilerParams(
-                collective_id=0, has_side_effects=True, vmem_limit_bytes=67_043_328
+                collective_id=0, has_side_effects=True, vmem_limit_bytes=67_043_328 - 4 * momentum.size
             ),
         )(grad_block, momentum, model_root.reshape(2, half, width), expert_root)
 

time: 113 us -> 110 us (0.973)
  local copies, waits for them, and re-layouts: 7.89 us -> 3.4 us
    unnamed x1, local copies, waits for them, and re-layouts: 7.89 us -> 3.4 us
where the time goes in v2:
time: 110 us; the launch traced here: 108 us
  Pallas kernels  105 us (95%)
  local copies, waits for them, and re-layouts  3.4 us (3%)
    pallas_call x1, Pallas kernels, per_device(): pl.pallas_call(functools.partial(kernel, n_blk, n_exp, n_chunks), out_sha...  105 us
    unnamed x1, local copies, waits for them, and re-layouts  3.4 us

profile of v2, /device:TPU:0, one launch (start us, length us, event | category | flops | bytes accessed | tf_op | source)
XLA Modules:
  0.0 108.0 jit_solution(6946994964012988618)
XLA Ops:
  0.0 104.6 %shard_map.46 = f32[32,32,2048]{2,1,0:T(8,128)S(1)} custom-call(bf16[32,32,2048]{2,1,0:T(8,128)(2,1)} %grad.1, f32[32,32,2048]{2,1,0:T(8,128)} %momentum.1, bf16[2,128,2048]{2,1,0:T(8,128)(2,1)} %bitcast.1, bf16[128,128]{1,0:T(8,128)(2,1)} %expert_root.1), custom_call_target="tpu_custom_call" | custom-call | tf_op jit(solution)/shard_map/pallas_call | solution.py:228
  104.6 3.4 %copy.6 = f32[32,32,2048]{2,1,0:T(8,128)} copy(f32[32,32,2048]{2,1,0:T(8,128)S(1)} %shard_map.46) | data formatting | bytes 16777216

commit v3 on v2

--- a/solution.py
+++ b/solution.py
@@ -14,10 +14,10 @@
 
 def kernel(
     n_blk, n_exp, n_chunks,
-    grad, momentum, root_rows, expert_root, out,
-    gathered, root, mix, blended,
+    grad, momentum, root_rows, expert_hbm, out,
+    expert_root, gathered, root, mix, blended,
     x_send, x_recv, p_send, p_recv, f_send, f_recv, own_sem,
-    z_send, z_recv, y_send, y_recv, c_send, c_recv, root_sem, mom_sem,
+    z_send, z_recv, y_send, y_recv, c_send, c_recv, root_sem, mom_sem, mix_sem,
 ):
     local_experts, local_hidden, width = grad.shape
     groups = local_hidden // SUB
@@ -100,6 +100,8 @@
     for p in range(1, len(pieces)):
         for off in range(1, chips):
             x_copy(p, off).start()
+    take_mix = pltpu.make_async_copy(expert_hbm, expert_root, mix_sem)
+    take_mix.start()
     for p in range(len(pieces)):
         own_copy(p).start()
         p_copy(p).start()
@@ -107,6 +109,7 @@
     for g in range(groups):
         mom_copy(g).start()
 
+    take_mix.wait()
     experts = expert_root.shape[1]
     spread = lax.broadcasted_iota(jnp.int32, (rows, local_experts), 0) // SUB
     spread = spread == lax.broadcasted_iota(jnp.int32, (rows, local_experts), 1)
@@ -171,7 +174,7 @@
 
     events = [functools.partial(take_z, d) for d in range(1, n_z)]
     events += [functools.partial(take_y, d) for d in range(n_z)]
-    ready = len(pieces) * 5 // 8
+    ready = len(pieces) * 11 // 16
     done = 0
     pending = 0
     for p, (g, c) in enumerate(pieces):
@@ -193,8 +196,8 @@
                 if d:
                     c_copy(0, d).wait_recv()
                 c_copy(1, d).wait_recv()
-        if p >= ready:
-            while pending <= p:
+        if p >= ready and p != len(pieces) - 3:
+            while pending <= p and (p > ready or pieces[pending][0] < g):
                 gg, first = pieces[pending]
                 last = c + 1 if gg == g else n_chunks
                 apply_root(gg, first, last)
@@ -228,9 +231,10 @@
         return pl.pallas_call(
             functools.partial(kernel, n_blk, n_exp, n_chunks),
             out_shape=pltpu.VMEM(momentum.shape, jnp.float32),
-            in_specs=[hbm, hbm, hbm, pl.BlockSpec(memory_space=pltpu.VMEM)],
+            in_specs=[hbm] * 4,
             out_specs=pl.BlockSpec(memory_space=pltpu.VMEM),
             scratch_shapes=[
+                pltpu.VMEM(expert_root.shape, jnp.bfloat16),
                 pltpu.VMEM((pieces, n_exp, local_experts, SUB, width // n_chunks), jnp.bfloat16),
                 pltpu.VMEM((n_blk, 2, half, width), jnp.bfloat16),
                 pltpu.VMEM((rows, experts * SUB), jnp.bfloat16),
@@ -242,7 +246,7 @@
                 dma((n_z - 1,)), dma((n_z - 1,)),
                 dma((n_z,)), dma((n_z,)),
                 dma((2, n_z)), dma((2, n_z)),
-                dma, dma((groups,)),
+                dma, dma((groups,)), dma,
             ],
             compiler_params=pltpu.CompilerParams(
                 collective_id=0, has_side_effects=True, vmem_limit_bytes=67_043_328 - 4 * momentum.size

time: 110 us -> 107 us (0.973); the launches traced: 108 us -> 107 us
  Pallas kernels: 105 us -> 103 us
    pallas_call x1, Pallas kernels: 105 us -> 103 us  [per_device(): pl.pallas_call(functools.partial(kernel, n_blk, n_exp, n_chunks), out_sha...]
where the time goes in v3:
time: 107 us
  Pallas kernels  103 us (96%)
  local copies, waits for them, and re-layouts  3.4 us (3%)
    pallas_call x1, Pallas kernels, per_device(): pl.pallas_call(functools.partial(kernel, n_blk, n_exp, n_chunks), out_sha...  103 us
    unnamed x1, local copies, waits for them, and re-layouts  3.4 us

profile of v3, /device:TPU:0, one launch (start us, length us, event | category | flops | bytes accessed | tf_op | source)
XLA Modules:
  0.0 106.6 jit_solution(10173260438514118974)
XLA Ops:
  0.0 103.2 %shard_map.46 = f32[32,32,2048]{2,1,0:T(8,128)S(1)} custom-call(bf16[32,32,2048]{2,1,0:T(8,128)(2,1)} %grad.1, f32[32,32,2048]{2,1,0:T(8,128)} %momentum.1, bf16[2,128,2048]{2,1,0:T(8,128)(2,1)} %bitcast.1, bf16[128,128]{1,0:T(8,128)(2,1)} %expert_hbm.1), custom_call_target="tpu_custom_call" | custom-call | tf_op jit(solution)/shard_map/pallas_call | solution.py:231
  103.2 3.4 %copy.6 = f32[32,32,2048]{2,1,0:T(8,128)} copy(f32[32,32,2048]{2,1,0:T(8,128)S(1)} %shard_map.46) | data formatting | bytes 16777216
